TPU v7x, 32 devices: a whole 2x2x4 slice. The times are simulated.
32 devices in a mesh: chain: 2 (over x), slab: 16 (over z, y, core).
Axes of the slice: x: 2, y: 2, z: 4, core: 2. Of those that a mesh axis runs over, the one named last changes fastest.
Arguments:
- whitened: float32 [1024, 256, 256], P(('chain', 'slab')), parts along dimension 0, may hold values from -6 to 6
- counts: int32 [1024, 256, 256], P(('chain', 'slab')), parts along dimension 0, may hold values from 0 to 24
- exposure: int32 [1024, 256, 256], P(('chain', 'slab')), parts along dimension 0, may hold values from 1 to 12
- cholesky_east: float32 [512, 512], replicated, as said below
- cholesky_north: float32 [256, 256], replicated, as said below
- cholesky_time: float32 [256, 256], replicated, as said below
Outputs:
- gradient: float32 [1024, 256, 256], P(('chain', 'slab')), parts along dimension 0
- density: float32 [2], P('chain'), parts along dimension 0
There are 2 independent parts, one for each index of `chain`. A program takes and returns all parts, laid end to end along the dimension named above; an argument that names none is the same for every part. Nothing has to cross between parts.
Inputs may be any that keep to these rules, and one draw needn't show every extreme that they name: `cholesky_east`: lower triangular with a positive diagonal, each row of unit length. `cholesky_north`: lower triangular with a positive diagonal, each row of unit length. `cholesky_time`: lower triangular with a positive diagonal, each row of unit length.
All inputs are finite; a program needn't handle non-finite values.
Results may differ from a plain program's by a relative error of at most 0.00008.
Values sent between devices are 32-bit elements; how exact they have to be, the bound alone decides.
A program may use at most 128 MiB of HBM per device.

v0:
```python
import jax
import jax.numpy as jnp
from jax import lax
from jax.sharding import PartitionSpec as P

field_scale = 0.6


def mode_last(values, matrix):
    return jnp.einsum("abc,tc->abt", values, matrix, precision=lax.Precision.HIGHEST)


def mode_middle(values, matrix):
    return jnp.einsum("abc,yb->ayc", values, matrix, precision=lax.Precision.HIGHEST)


def mode_first(values, matrix):
    return jnp.einsum("abc,xa->xbc", values, matrix, precision=lax.Precision.HIGHEST)


def adjoint_last(values, matrix):
    return jnp.einsum("abt,tc->abc", values, matrix, precision=lax.Precision.HIGHEST)


def adjoint_middle(values, matrix):
    return jnp.einsum("ayc,yb->abc", values, matrix, precision=lax.Precision.HIGHEST)


def adjoint_first(values, matrix):
    return jnp.einsum("xbc,xa->abc", values, matrix, precision=lax.Precision.HIGHEST)


def to_lines(values):
    return lax.all_to_all(values, "slab", split_axis=1, concat_axis=0, tiled=True)


def to_planes(values):
    return lax.all_to_all(values, "slab", split_axis=0, concat_axis=1, tiled=True)


def per_device(whitened, counts, exposure, cholesky_east, cholesky_north, cholesky_time):
    cell_count = whitened.shape[0] * whitened.shape[1] * whitened.shape[2]
    prior_term = -0.5 * jnp.sum(whitened * whitened)
    partly = mode_middle(mode_last(whitened, cholesky_time), cholesky_north)
    counts_lines, exposure_lines = (
        lax.all_to_all(counts, "slab", split_axis=1, concat_axis=0, tiled=True),
        lax.all_to_all(exposure, "slab", split_axis=1, concat_axis=0, tiled=True),
    )
    log_lines = field_scale * mode_first(to_lines(partly), cholesky_east)
    observed = counts_lines.astype(jnp.float32)
    intensity = exposure_lines.astype(jnp.float32) * jnp.exp(log_lines)
    residual = observed - intensity
    partial_sum = jnp.sum(observed * log_lines - intensity) + prior_term
    adjoint_lines = adjoint_first(residual, cholesky_east)
    adjoint = to_planes(adjoint_lines)
    adjoint = adjoint_last(adjoint_middle(adjoint, cholesky_north), cholesky_time)
    gradient = field_scale * adjoint - whitened
    total_sum = lax.psum(partial_sum, "slab")
    density = total_sum / (cell_count * lax.axis_size("slab"))
    return (gradient, jnp.reshape(density, (1,)))


def solution(mesh):
    placed = (
        P(("chain", "slab"), None, None),
        P(("chain", "slab"), None, None),
        P(("chain", "slab"), None, None),
        P(),
        P(),
        P(),
    )
    return jax.shard_map(
        per_device,
        mesh=mesh,
        in_specs=placed,
        out_specs=(P(("chain", "slab"), None, None), P("chain")),
        check_vma=False,
    )
```

profile of v0, /device:TPU:1, one launch (start us, length us, event | category | flops | bytes accessed | tf_op | source)
XLA Modules:
  0.0 894.7 jit_solution(4330136956723541852)
XLA Ops:
  0.6 0.0 copy-start
  0.6 11.5 %copy.35 = s32[32,256,256]{2,0,1:T(8,128)} copy(s32[32,256,256]{2,1,0:T(8,128)} %param.8) | data formatting | bytes 16777216 | tf_op args[2]
  12.2 7.3 all-to-all-start.1
  19.5 11.6 %copy.32 = s32[32,256,256]{2,0,1:T(8,128)} copy(s32[32,256,256]{2,1,0:T(8,128)} %param.7) | data formatting | bytes 16777216 | tf_op args[1]
  31.2 0.0 copy-start.2
  31.2 139.5 %all-to-all-done.1 = s32[32,256,256]{2,0,1:T(8,128)} async-done(((s32[32,256,256]{2,0,1:T(8,128)}), s32[32,256,256]{2,0,1:T(8,128)}, u32[]{:S(2)}, u32[]{:S(2)}) %all-to-all-start.1) | async-done | bytes 8388640 | tf_op jit(solution)/shard_map/all_to_all | solution.py:47
  170.7 36.3 %all-to-all-start = ((s32[32,256,256]{2,0,1:T(8,128)}), s32[32,256,256]{2,0,1:T(8,128)}, u32[]{:S(2)}, u32[]{:S(2)}) async-start(s32[32,256,256]{2,0,1:T(8,128)} %copy.32), calls=%async_computation | async-start | bytes 16777216 | tf_op jit(solution)/shard_map/all_to_all | solution.py:46
  207.0 0.0 copy-done.2
  207.0 0.0 copy-start.1
  207.0 10.7 %fusion.22 = f32[32,256,256]{1,2,0:T(8,128)S(1)} fusion(f32[32,256,256]{2,1,0:T(8,128)} %param.6, f32[256,256]{1,0:T(8,128)S(1)} %copy-done.2), kind=kOutput, calls=%fused_computation.24 | convolution fusion | flops 6442450944 | bytes 17039360 | tf_op jit(solution)/shard_map/abc,tc->abt/dot_general | solution.py:10
  217.8 0.0 copy-done.1
  217.8 8.9 convolution_bitcast_fusion
  226.7 10.3 %copy.39 = f32[32,256,256]{2,0,1:T(8,128)} copy(f32[32,256,256]{1,2,0:T(8,128)} %convolution_bitcast_fusion) | data formatting | bytes 16777216 | tf_op jit(solution)/shard_map/abc,yb->ayc/transpose | solution.py:14
  237.0 121.1 %all-to-all-done = s32[32,256,256]{2,0,1:T(8,128)} async-done(((s32[32,256,256]{2,0,1:T(8,128)}), s32[32,256,256]{2,0,1:T(8,128)}, u32[]{:S(2)}, u32[]{:S(2)}) %all-to-all-start) | async-done | bytes 8388640 | tf_op jit(solution)/shard_map/all_to_all | solution.py:46
  358.0 36.3 %all-to-all-start.2 = ((f32[32,256,256]{2,0,1:T(8,128)}), f32[32,256,256]{2,0,1:T(8,128)}, u32[]{:S(2)}, u32[]{:S(2)}) async-start(f32[32,256,256]{2,0,1:T(8,128)} %copy.39), calls=%async_computation.2 | async-start | bytes 16777216 | tf_op jit(solution)/shard_map/all_to_all | solution.py:34
  394.4 8.2 copy_convert_fusion
  402.6 4.4 copy.37
  407.0 10.4 %copy.43 = f32[512,16,256]{0,2,1:T(8,128)} copy(f32[512,16,256]{2,1,0:T(8,128)} %bitcast.68) | data formatting | bytes 16777216 | tf_op jit(solution)/shard_map/convert_element_type | solution.py:51
  417.4 8.2 copy_convert_fusion.1
  425.7 4.4 copy.34
  430.1 10.1 %copy.44 = f32[512,16,256]{0,2,1:T(8,128)} copy(f32[512,16,256]{2,1,0:T(8,128)} %bitcast.70) | data formatting | bytes 16777216 | tf_op jit(solution)/shard_map/convert_element_type | solution.py:50
  440.2 105.2 %all-to-all-done.2 = f32[32,256,256]{2,0,1:T(8,128)} async-done(((f32[32,256,256]{2,0,1:T(8,128)}), f32[32,256,256]{2,0,1:T(8,128)}, u32[]{:S(2)}, u32[]{:S(2)}) %all-to-all-start.2) | async-done | bytes 8388640 | tf_op jit(solution)/shard_map/all_to_all | solution.py:34
  545.4 0.0 slice-start.2
  545.4 13.6 %copy.41 = f32[16,32,16,256]{3,2,1,0:T(8,128)} copy(f32[16,32,16,256]{3,1,2,0:T(8,128)} %bitcast.11) | data formatting | bytes 16777216 | tf_op jit(solution)/shard_map/all_to_all | solution.py:34
  559.0 0.0 copy-done
  559.0 0.0 slice-start.3
  559.0 37.1 %fusion.4 = (f32[]{:T(128)}, f32[16,256,512]{2,1,0:T(8,128)}) fusion(f32[512,16,256]{0,2,1:T(8,128)} %copy.44, f32[512,16,256]{0,2,1:T(8,128)} %copy.43, f32[512,512]{1,0:T(8,128)S(1)} %copy-done, f32[512,16,256]{2,1,0:T(8,128)} %bitcast.66), kind=kOutput, calls=%fused_computation.6 | convolution fusion | flops 12895387648 | bytes 34603012 | tf_op jit(solution)/shard_map/abc,xa->xbc/dot_general | solution.py:18
  596.1 0.0 slice-done.2
  596.1 0.0 slice-done.3
  596.1 20.3 %fusion.13 = f32[512,16,256]{0,2,1:T(8,128)} fusion(f32[512,16,256]{0,2,1:T(8,128)} %copy.44, f32[512,16,256]{0,2,1:T(8,128)S(1)} %bitcast.65, f32[16,256,512]{2,1,0:T(8,128)} %get-tuple-element.3, f32[512,512]{1,0:T(8,128)S(1)} %copy-done), kind=kOutput, calls=%fused_computation.17 | convolution fusion | flops 12891193344 | bytes 34603008 | tf_op jit(solution)/shard_map/xbc,xa->abc/dot_general | solution.py:30
  616.4 10.3 %copy.45 = f32[512,16,256]{2,1,0:T(8,128)} copy(f32[512,16,256]{0,2,1:T(8,128)} %fusion.13) | data formatting | bytes 16777216 | tf_op jit(solution)/shard_map/xbc,xa->abc/dot_general | solution.py:30
  626.6 36.0 %all-to-all-start.3 = ((f32[512,16,256]{2,1,0:T(8,128)}), f32[512,16,256]{2,1,0:T(8,128)}, u32[]{:S(2)}, u32[]{:S(2)}) async-start(f32[512,16,256]{2,1,0:T(8,128)} %copy.45), calls=%async_computation.3 | async-start | bytes 16777216 | tf_op jit(solution)/shard_map/all_to_all | solution.py:38
  662.6 6.1 multiply_reduce_fusion
  670.0 187.1 %psum.7 = f32[]{:T(128)} all-reduce(f32[]{:T(128)S(6)} %add.5), channel_id=1, replica_groups=mesh['chain'=2,'slab'=16] {'slab'}, use_global_device_ids=true, to_apply=%region_2.0 | all-reduce | flops 1 | bytes 8 | tf_op jit(solution)/shard_map/psum | solution.py:58
  857.7 0.0 all-to-all-done.3
  857.8 0.0 slice-start
  857.8 4.6 copy.46
  862.3 0.0 slice-start.1
  862.3 14.6 %fusion.18 = f32[32,256,256]{2,1,0:T(8,128)S(1)} fusion(f32[32,256,256]{2,1,0:T(8,128)S(1)} %bitcast.71, f32[256,256]{1,0:T(8,128)S(1)} %copy-done.1), kind=kOutput, calls=%fused_computation.20 | convolution fusion | flops 6442450944 | bytes 17039360 | tf_op jit(solution)/shard_map/ayc,yb->abc/dot_general | solution.py:26
  876.9 0.0 slice-done
  876.9 0.0 slice-done.1
  877.0 16.3 %multiply_subtract_fusion = f32[32,256,256]{2,1,0:T(8,128)} fusion(f32[32,256,256]{2,1,0:T(8,128)S(1)} %bitcast.63, f32[32,256,256]{2,1,0:T(8,128)S(1)} %fusion.18, f32[256,256]{1,0:T(8,128)S(1)} %copy-done.2), kind=kOutput, calls=%fused_computation.12 | convolution fusion | flops 6446645248 | bytes 25427968 | tf_op jit(solution)/shard_map/abt,tc->abc/dot_general | solution.py:22
  (2 shorter events, 0.0 us)
Async XLA Ops:
  0.6 558.4 %copy-start = (f32[512,512]{1,0:T(8,128)S(1)}, f32[512,512]{1,0:T(8,128)}, u32[]{:S(2)}) copy-start(f32[512,512]{1,0:T(8,128)} %param.9) | copy-start | bytes 3145732
  12.2 158.5 %all-to-all-start.1 = ((s32[32,256,256]{2,0,1:T(8,128)}), s32[32,256,256]{2,0,1:T(8,128)}, u32[]{:S(2)}, u32[]{:S(2)}) async-start(s32[32,256,256]{2,0,1:T(8,128)} %copy.35), calls=%async_computation.1 | async-start | bytes 16777216 | tf_op jit(solution)/shard_map/all_to_all | solution.py:47
  31.2 175.9 %copy-start.2 = (f32[256,256]{1,0:T(8,128)S(1)}, f32[256,256]{1,0:T(8,128)}, u32[]{:S(2)}) copy-start(f32[256,256]{1,0:T(8,128)} %param.11) | copy-start | bytes 786436
  170.7 187.3 %all-to-all-start = ((s32[32,256,256]{2,0,1:T(8,128)}), s32[32,256,256]{2,0,1:T(8,128)}, u32[]{:S(2)}, u32[]{:S(2)}) async-start(s32[32,256,256]{2,0,1:T(8,128)} %copy.32), calls=%async_computation | async-start | bytes 16777216 | tf_op jit(solution)/shard_map/all_to_all | solution.py:46
  207.0 10.7 %copy-start.1 = (f32[256,256]{1,0:T(8,128)S(1)}, f32[256,256]{1,0:T(8,128)}, u32[]{:S(2)}) copy-start(f32[256,256]{1,0:T(8,128)} %param.10) | copy-start | bytes 786436
  358.0 187.4 %all-to-all-start.2 = ((f32[32,256,256]{2,0,1:T(8,128)}), f32[32,256,256]{2,0,1:T(8,128)}, u32[]{:S(2)}, u32[]{:S(2)}) async-start(f32[32,256,256]{2,0,1:T(8,128)} %copy.39), calls=%async_computation.2 | async-start | bytes 16777216 | tf_op jit(solution)/shard_map/all_to_all | solution.py:34
  545.4 50.7 %slice-start.2 = ((s8[8388608]{0:T(1024)(128)(4,1)}), s8[4194304]{0:T(1024)(128)(4,1)S(1)}, s32[]{:S(2)}) async-start(s8[8388608]{0:T(1024)(128)(4,1)} %bitcast.64), calls=%async_computation.6 | async-start | bytes 8388608
  559.0 37.1 %slice-start.3 = ((s8[8388608]{0:T(1024)(128)(4,1)}), s8[4194304]{0:T(1024)(128)(4,1)S(1)}, s32[]{:S(2)}) async-start(s8[8388608]{0:T(1024)(128)(4,1)} %bitcast.64), calls=%async_computation.7 | async-start | bytes 8388608
  626.6 231.1 %all-to-all-start.3 = ((f32[512,16,256]{2,1,0:T(8,128)}), f32[512,16,256]{2,1,0:T(8,128)}, u32[]{:S(2)}, u32[]{:S(2)}) async-start(f32[512,16,256]{2,1,0:T(8,128)} %copy.45), calls=%async_computation.3 | async-start | bytes 16777216 | tf_op jit(solution)/shard_map/all_to_all | solution.py:38
  857.8 19.2 %slice-start = ((s8[8388608]{0:T(1024)(128)(4,1)}), s8[4194304]{0:T(1024)(128)(4,1)S(1)}, s32[]{:S(2)}) async-start(s8[8388608]{0:T(1024)(128)(4,1)} %bitcast.62), calls=%async_computation.4 | async-start | bytes 8388608
  862.3 14.6 %slice-start.1 = ((s8[8388608]{0:T(1024)(128)(4,1)}), s8[4194304]{0:T(1024)(128)(4,1)S(1)}, s32[]{:S(2)}) async-start(s8[8388608]{0:T(1024)(128)(4,1)} %bitcast.62), calls=%async_computation.5 | async-start | bytes 8388608
where the time goes:
time: 909 us; the launch traced here: 895 us
  waiting for transfers between devices  366 us (40%)
  blocking collectives  187 us (21%)
  starting transfers between devices  116 us (13%)
  matrix products  108 us (12%)
  local copies, waits for them, and re-layouts  91.2 us (10%)
  other arithmetic  22.6 us (2%)
    psum x1, blocking collectives, per_device(): total_sum = lax.psum(partial_sum, 'slab')  187 us
    all_to_all x1, waiting for transfers between devices, per_device(): lax.all_to_all(exposure, 'slab', split_axis=1, concat_axis=0, tiled=True)  140 us
    all_to_all x1, waiting for transfers between devices, per_device(): lax.all_to_all(counts, 'slab', split_axis=1, concat_axis=0, tiled=True)  121 us
    all_to_all x1, waiting for transfers between devices, to_lines(): lax.all_to_all(values, 'slab', split_axis=1, concat_axis=0, tiled=True)  105 us
    dot_general x1, matrix products, mode_first(): jnp.einsum('abc,xa->xbc', values, matrix, precision=lax.Precision.HIGHEST)  37.1 us
    all_to_all x1, starting transfers between devices, to_lines(): lax.all_to_all(values, 'slab', split_axis=1, concat_axis=0, tiled=True)  36.3 us
    all_to_all x1, starting transfers between devices, per_device(): lax.all_to_all(counts, 'slab', split_axis=1, concat_axis=0, tiled=True)  36.3 us
    all_to_all x1, starting transfers between devices, to_planes(): lax.all_to_all(values, 'slab', split_axis=0, concat_axis=1, tiled=True)  36 us
  transfers between devices with their start and end apart: 4, of which 3 were waited for; matrix products, arithmetic and copies ran while one was open for 10% of the time, Pallas kernels for 0%

commit v1 on v0

v1 whole, which is shorter than its diff:
```python
import functools

import jax
import jax.numpy as jnp
from jax import lax
from jax.experimental import pallas as pl
from jax.experimental.pallas import tpu as pltpu
from jax.sharding import PartitionSpec as P

field_scale = 0.6
QUARTERS = 4
MAX_CHUNKS = 16
AHEAD = 3
VMEM_BYTES = 67043328
HIGH = lax.Precision.HIGH


def split(values):
    high = values.astype(jnp.bfloat16)
    low = (values - high.astype(jnp.float32)).astype(jnp.bfloat16)
    return high, low


def dot(left, right):
    return jnp.dot(left, right, preferred_element_type=jnp.float32)


def kernel(
    group, chunks, q_hbm, cnt_hbm, exp_hbm, lh, ll, th, tl, out_hbm, acc,
    own, f0, f1, res, wgt, b0, b1,
    send_in, recv_p, recv_c, recv_e, send_z, recv_f0, recv_f1, recv_b0, recv_b1, send_g, recv_g,
):
    slab = lax.axis_index("slab")
    quarter = slab // group
    place = slab % group
    lines = own.shape[0]
    rows = own.shape[1]
    planes = q_hbm.shape[1]
    step = lines // chunks

    def device(quarter_of, place_of):
        return {"slab": quarter_of * group + place_of}

    barrier = pltpu.get_barrier_semaphore()
    for j in range(1, group):
        pl.semaphore_signal(barrier, inc=1, device_id=device(quarter, lax.rem(place + j, group)), device_id_type=pl.DeviceIdType.MESH)
    for j in range(1, QUARTERS):
        pl.semaphore_signal(barrier, inc=1, device_id=device(lax.rem(quarter + j, QUARTERS), place), device_id_type=pl.DeviceIdType.MESH)
    pl.semaphore_wait(barrier, group + QUARTERS - 2)

    acc[...] = jnp.zeros_like(acc)

    def part(chunk):
        return pl.ds(chunk * step, step)

    def remote(src, dst, send_sem, recv_sem, target):
        pltpu.make_async_remote_copy(
            src_ref=src, dst_ref=dst, send_sem=send_sem, recv_sem=recv_sem,
            device_id=target, device_id_type=pl.DeviceIdType.MESH,
        ).start()

    def await_bytes(ref, sem):
        pltpu.make_async_copy(ref, ref, sem).wait()

    def spread(chunk):
        mine = pl.ds(place * planes, planes)
        for k, (src, dst, recv) in enumerate(((q_hbm, own, recv_p), (cnt_hbm, res, recv_c), (exp_hbm, wgt, recv_e))):
            for j in range(1, group):
                to = lax.rem(place + j, group)
                remote(
                    src.at[pl.ds(to * lines + chunk * step, step)], dst.at[part(chunk), mine],
                    send_in.at[k], recv.at[chunk], device(quarter, to),
                )
            pltpu.make_async_copy(
                src.at[pl.ds(place * lines + chunk * step, step)], dst.at[part(chunk), mine], recv.at[chunk]
            ).start()

    def collect(chunk):
        for j in range(1, group):
            to = lax.rem(place + j, group)
            remote(
                wgt.at[part(chunk), pl.ds(to * planes, planes)],
                out_hbm.at[pl.ds(place * lines + chunk * step, step)],
                send_g, recv_g, device(quarter, to),
            )
        pltpu.make_async_copy(
            wgt.at[part(chunk), pl.ds(place * planes, planes)],
            out_hbm.at[pl.ds(place * lines + chunk * step, step)], recv_g,
        ).start()

    def product(high, low, row, terms, y, base=None):
        total = base
        for col, (x_high, x_low) in terms:
            block = (slice(row * rows, (row + 1) * rows), slice(col * rows, (col + 1) * rows))
            a_high, a_low = high[block], low[block]
            value = dot(a_high, x_high) + (dot(a_high, x_low) + dot(a_low, x_high))
            total = value if total is None else total + value
        return total

    def observe(y, field):
        log_rate = field_scale * field
        observed = res[y]
        intensity = wgt[y] * jnp.exp(log_rate)
        acc[...] += observed * log_rate - intensity
        res[y] = observed - intensity

    def over_lines(chunk, body):
        def at_line(i, carry):
            body(chunk * step + i)
            return carry

        lax.fori_loop(0, step, at_line, 0, unroll=min(step, 2))

    def forward(q, chunk):
        await_bytes(res.at[part(chunk)], recv_c.at[chunk])
        await_bytes(wgt.at[part(chunk)], recv_e.at[chunk])
        if q >= 1:
            await_bytes(f0.at[part(chunk)], recv_f0.at[chunk])
        if q == 2:
            await_bytes(f1.at[part(chunk)], recv_f1.at[chunk])

        def line(y):
            terms = [(q, split(own[y]))]
            if q in (1, 2):
                terms.append((q - 1, split(f0[y])))
            if q == 2:
                terms.append((0, split(f1[y])))
            observe(y, product(lh, ll, q, terms, y, f0[y] if q == 3 else None))
            if q == 2:
                b1[y] = product(lh, ll, 3, terms, y)

        over_lines(chunk, line)
        if q == 2:
            remote(b1.at[part(chunk)], f0.at[part(chunk)], send_z.at[0], recv_f0.at[chunk], device(3, place))
            remote(res.at[part(chunk)], b0.at[part(chunk)], send_z.at[1], recv_b0.at[chunk], device(1, place))
        if q == 3:
            remote(res.at[part(chunk)], b0.at[part(chunk)], send_z.at[0], recv_b0.at[chunk], device(2, place))
            remote(res.at[part(chunk)], b1.at[part(chunk)], send_z.at[1], recv_b1.at[chunk], device(1, place))

    def backward(q, chunk):
        if q <= 2:
            await_bytes(b0.at[part(chunk)], recv_b0.at[chunk])
        if q == 1:
            await_bytes(b1.at[part(chunk)], recv_b1.at[chunk])

        def line(y):
            terms = [(q, split(res[y]))]
            if q in (1, 2):
                terms.append((q + 1, split(b0[y])))
            if q == 1:
                terms.append((3, split(b1[y])))
            wgt[y] = product(th, tl, q, terms, y, b0[y] if q == 0 else None)
            if q == 1:
                f1[y] = product(th, tl, 0, terms, y)

        over_lines(chunk, line)
        if q == 1:
            remote(f1.at[part(chunk)], b0.at[part(chunk)], send_z.at[1], recv_b0.at[chunk], device(0, place))

    def onward(q, chunk):
        await_bytes(own.at[part(chunk)], recv_p.at[chunk])
        if q == 0:
            remote(own.at[part(chunk)], f0.at[part(chunk)], send_z.at[0], recv_f0.at[chunk], device(1, place))
            remote(own.at[part(chunk)], f1.at[part(chunk)], send_z.at[1], recv_f1.at[chunk], device(2, place))
        if q == 1:
            remote(own.at[part(chunk)], f0.at[part(chunk)], send_z.at[0], recv_f0.at[chunk], device(2, place))

    ahead = min(AHEAD, chunks)
    for chunk in range(ahead):
        spread(chunk)

    forward_lag = (1, 1, 1, 2)
    backward_lag = (4, 3, 3, 2)

    def turn(i, carry):
        @pl.when(i + ahead < chunks)
        def _():
            spread(i + ahead)

        for q in range(QUARTERS):
            @pl.when((quarter == q) & (i < chunks))
            def _(q=q):
                onward(q, i)

            @pl.when((quarter == q) & (i >= forward_lag[q]) & (i < chunks + forward_lag[q]))
            def _(q=q):
                forward(q, i - forward_lag[q])

            @pl.when((quarter == q) & (i >= backward_lag[q]) & (i < chunks + backward_lag[q]))
            def _(q=q):
                backward(q, i - backward_lag[q])
                collect(i - backward_lag[q])

        return carry

    lax.fori_loop(0, chunks + max(backward_lag), turn, 0)

    away = pl.ds(0, (group - 1) * lines)
    if group > 1:
        for k, src in enumerate((q_hbm, cnt_hbm, exp_hbm)):
            await_bytes(src.at[away], send_in.at[k])
        await_bytes(out_hbm.at[away], send_g)
    for k in range(2):
        await_bytes(own, send_z.at[k])
    await_bytes(out_hbm, recv_g)


def exchange(partly, counts, exposure, east, group):
    lines = partly.shape[0] // group
    rows = partly.shape[1] * group
    times = partly.shape[2]
    chunks = min(MAX_CHUNKS, lines)
    rounded = lax.reduce_precision(east, 8, 7)
    high, low = rounded.astype(jnp.bfloat16), (east - rounded).astype(jnp.bfloat16)
    whole = lambda: pltpu.VMEM((lines, rows, times), jnp.float32)
    any_space = pl.BlockSpec(memory_space=pl.ANY)
    in_vmem = pl.BlockSpec(memory_space=pltpu.VMEM)
    dma = pltpu.SemaphoreType.DMA
    return pl.pallas_call(
        functools.partial(kernel, group, chunks),
        out_shape=(
            jax.ShapeDtypeStruct(partly.shape, jnp.float32),
            jax.ShapeDtypeStruct((rows, times), jnp.float32),
        ),
        in_specs=[any_space] * 3 + [in_vmem] * 4,
        out_specs=(any_space, in_vmem),
        scratch_shapes=[whole() for _ in range(7)]
        + [dma((3,))]
        + [dma((chunks,)) for _ in range(3)]
        + [dma((2,))]
        + [dma((chunks,)) for _ in range(4)]
        + [dma, dma],
        compiler_params=pltpu.CompilerParams(
            collective_id=0, has_side_effects=True, vmem_limit_bytes=VMEM_BYTES
        ),
    )(partly, counts, exposure, high, low, high.T, low.T)


def per_device(whitened, counts, exposure, cholesky_east, cholesky_north, cholesky_time):
    slabs = lax.axis_size("slab")
    cell_count = whitened.shape[0] * whitened.shape[1] * whitened.shape[2]
    prior_term = -0.5 * jnp.sum(whitened * whitened)
    partly = jnp.einsum("abc,tc->abt", whitened, cholesky_time, precision=HIGH)
    partly = jnp.einsum("abt,yb->yat", partly, cholesky_north, precision=HIGH)
    counts_lines = jnp.transpose(counts.astype(jnp.float32), (1, 0, 2))
    exposure_lines = jnp.transpose(exposure.astype(jnp.float32), (1, 0, 2))
    adjoint, terms = exchange(partly, counts_lines, exposure_lines, cholesky_east, slabs // QUARTERS)
    adjoint = jnp.einsum("yat,yb->abt", adjoint, cholesky_north, precision=HIGH)
    adjoint = jnp.einsum("abt,tc->abc", adjoint, cholesky_time, precision=HIGH)
    gradient = field_scale * adjoint - whitened
    total_sum = lax.psum(jnp.sum(terms) + prior_term, "slab")
    density = total_sum / (cell_count * slabs)
    return (gradient, jnp.reshape(density, (1,)))


def solution(mesh):
    placed = (
        P(("chain", "slab"), None, None),
        P(("chain", "slab"), None, None),
        P(("chain", "slab"), None, None),
        P(),
        P(),
        P(),
    )
    return jax.shard_map(
        per_device,
        mesh=mesh,
        in_specs=placed,
        out_specs=(P(("chain", "slab"), None, None), P("chain")),
        check_vma=False,
    )
```

time: 909 us -> 544 us (0.60); the launches traced: 895 us -> 542 us
  Pallas kernels: 0 us -> 436 us
  waiting for transfers between devices: 366 us -> 0 us
  blocking collectives: 187 us -> 29 us
  starting transfers between devices: 116 us -> 0 us
  local copies, waits for them, and re-layouts: 91.2 us -> 14 us
  matrix products: 108 us -> 31.7 us
    pallas_call x0 -> x1, Pallas kernels: none -> 436 us  [exchange(): pl.pallas_call(functools.partial(kernel, group, chunks), out_shape=(jax.S...]
    all_to_all x4 -> x0, waiting for transfers between devices: 366 us -> none  [the longest x1 140 us: per_device(): lax.all_to_all(exposure, 'slab', split_axis=1, concat_axis=0, tiled=True)]
    psum x1, blocking collectives: 187 us -> 29 us  [per_device(): total_sum = lax.psum(jnp.sum(terms) + prior_term, 'slab')]
    all_to_all x4 -> x0, starting transfers between devices: 116 us -> none  [the longest x1 36.3 us: to_lines(): lax.all_to_all(values, 'slab', split_axis=1, concat_axis=0, tiled=True)]
    dot_general x6 -> x4, matrix products: 108 us -> 31.7 us  [the longest x1 11.9 us: per_device(): adjoint = jnp.einsum('yat,yb->abt', adjoint, cholesky_north, precision=HIGH)]
    convert_element_type x4 -> x2, local copies, waits for them, and re-layouts: 29.3 us -> 2.16 us  [the longest x1 1.13 us: exchange(): rounded.astype(jnp.bfloat16)]
    unnamed x16 -> x13, local copies, waits for them, and re-layouts: 23.2 us -> 1.58 us
    transpose x0 -> x1, other arithmetic: none -> 19.7 us  [per_device(): exposure_lines = jnp.transpose(exposure.astype(jnp.float32), (1, 0, 2))]
  transfers between devices with their start and end apart: 4 -> 0, of which waited for: 3 -> 0; matrix products, arithmetic and copies ran while one was open for 10% -> 0% of each run, Pallas kernels for 0% -> 0%
where the time goes in v1:
time: 544 us; the launch traced here: 542 us
  Pallas kernels  436 us (80%)
  matrix products  31.7 us (6%)
  blocking collectives  29 us (5%)
  other arithmetic  26.6 us (5%)
  local copies, waits for them, and re-layouts  14 us (3%)
    pallas_call x1, Pallas kernels, exchange(): pl.pallas_call(functools.partial(kernel, group, chunks), out_shape=(jax.S...  436 us
    psum x1, blocking collectives, per_device(): total_sum = lax.psum(jnp.sum(terms) + prior_term, 'slab')  29 us
    transpose x1, other arithmetic, per_device(): exposure_lines = jnp.transpose(exposure.astype(jnp.float32), (1, 0, 2))  19.7 us
    dot_general x1, matrix products, per_device(): adjoint = jnp.einsum('yat,yb->abt', adjoint, cholesky_north, precision=HIGH)  11.9 us

profile of v1, /device:TPU:1, one launch (start us, length us, event | category | flops | bytes accessed | tf_op | source)
XLA Modules:
  0.0 541.6 jit_solution(16089630560367395451)
XLA Ops:
  0.6 1.6 copy.11
  2.2 0.2 fusion.8
  2.4 0.0 copy-start
  2.4 0.0 copy-start.1
  2.4 1.1 copy.13.lh
  3.5 1.0 copy.14.ll
  4.5 0.0 copy-start.3
  4.5 19.7 %fusion.4 = (f32[256,32,256]{2,1,0:T(8,128)}, f32[256,32,256]{2,1,0:T(8,128)}) fusion(s32[32,256,256]{2,1,0:T(8,128)} %param.8, s32[32,256,256]{2,1,0:T(8,128)} %param.7), kind=kLoop, calls=%fused_computation.5 | loop fusion | flops 4194304 | bytes 33554432 | tf_op jit(solution)/shard_map/transpose | solution.py:246
  24.2 0.0 copy-done
  24.2 0.0 copy-done.1
  24.2 0.0 copy-done.3
  24.2 0.0 copy-start.2
  24.3 6.2 %fusion.13 = f32[32,256,256]{1,2,0:T(8,128)S(1)} fusion(f32[32,256,256]{2,1,0:T(8,128)} %param.6, f32[256,256]{1,0:T(8,128)S(1)} %copy-done.3), kind=kOutput, calls=%fused_computation.17 | convolution fusion | flops 3221225472 | bytes 17039360 | tf_op jit(solution)/shard_map/abc,tc->abt/dot_general | solution.py:243
  30.4 0.0 copy-done.2
  30.4 5.7 %fusion.10 = f32[32,256,256]{2,1,0:T(8,128)} fusion(f32[32,256,256]{1,2,0:T(8,128)S(1)} %fusion.13, f32[256,256]{1,0:T(8,128)S(1)} %copy-done.2), kind=kOutput, calls=%fused_computation.14 | convolution fusion | flops 3221225472 | bytes 17039360 | tf_op jit(solution)/shard_map/abt,yb->yat/dot_general | solution.py:244
  36.2 10.3 %copy.8 = f32[32,256,256]{1,0,2:T(8,128)} copy(f32[32,256,256]{2,1,0:T(8,128)} %fusion.10) | data formatting | bytes 16777216 | tf_op jit(solution)/shard_map/abt,yb->yat/dot_general | solution.py:244
  46.4 436.5 %shard_map.77 = (f32[256,32,256]{2,1,0:T(8,128)}, f32[128,256]{1,0:T(8,128)}) custom-call(f32[256,32,256]{2,1,0:T(8,128)} %bitcast.25, f32[256,32,256]{2,1,0:T(8,128)} %get-tuple-element.9.cnt_hbm, f32[256,32,256]{2,1,0:T(8,128)} %get-tuple-element.8.exp_hbm, bf16[512,512]{1,0:T(8,128)(2,1)} %copy.13.lh, bf16[512,512]{1,0:T(8,128)(2,1)} %copy.14.ll, ...), custom_call_target="tpu_custom_call" | custom-call | tf_op jit(solution)/shard_map/pallas_call | solution.py:219
  482.9 0.0 copy-start.4
  482.9 11.9 %fusion.2 = f32[32,256,256]{1,2,0:T(8,128)S(1)} fusion(f32[256,32,256]{2,1,0:T(8,128)} %get-tuple-element.4, f32[256,256]{1,0:T(8,128)} %param.10), kind=kOutput, calls=%fused_computation.2 | convolution fusion | flops 3221225472 | bytes 17039360 | tf_op jit(solution)/shard_map/yat,yb->abt/dot_general | solution.py:248
  494.9 0.0 copy-done.4
  494.9 0.0 copy-start.5
  494.9 7.9 %multiply_subtract_fusion = f32[32,256,256]{2,1,0:T(8,128)} fusion(f32[32,256,256]{2,1,0:T(8,128)} %param.6, f32[32,256,256]{1,2,0:T(8,128)S(1)} %fusion.2, f32[256,256]{1,0:T(8,128)S(1)} %copy-done.4), kind=kOutput, calls=%fused_computation.9 | convolution fusion | flops 3225419776 | bytes 25427968 | tf_op jit(solution)/shard_map/abt,tc->abc/dot_general | solution.py:249
  502.8 0.0 copy-done.5
  502.8 0.6 reduce_sum.18
  503.4 6.1 %multiply_reduce_fusion = f32[]{:T(128)} fusion(f32[32,256,256]{2,1,0:T(8,128)} %param.6), kind=kLoop, calls=%fused_computation.8 | loop fusion | flops 4194303 | bytes 8388612 | tf_op jit(solution)/shard_map/reduce_sum | solution.py:242
  510.8 29.0 %psum.7 = f32[]{:T(128)} all-reduce(f32[]{:T(128)S(6)} %add.5), channel_id=1, replica_groups=mesh['chain'=2,'slab'=16] {'slab'}, use_global_device_ids=true, to_apply=%region_2.0 | all-reduce | flops 1 | bytes 8 | tf_op jit(solution)/shard_map/psum | solution.py:251
Async XLA Ops:
  2.4 21.9 %copy-start = (bf16[512,512]{0,1:T(8,128)(2,1)}, bf16[512,512]{0,1:T(8,128)(2,1)S(1)}, u32[]{:S(2)}) copy-start(bf16[512,512]{0,1:T(8,128)(2,1)S(1)} %get-tuple-element.6) | copy-start | bytes 1572868
  2.4 21.9 %copy-start.1 = (bf16[512,512]{0,1:T(8,128)(2,1)}, bf16[512,512]{0,1:T(8,128)(2,1)S(1)}, u32[]{:S(2)}) copy-start(bf16[512,512]{0,1:T(8,128)(2,1)S(1)} %get-tuple-element.7) | copy-start | bytes 1572868
  4.5 19.7 %copy-start.3 = (f32[256,256]{1,0:T(8,128)S(1)}, f32[256,256]{1,0:T(8,128)}, u32[]{:S(2)}) copy-start(f32[256,256]{1,0:T(8,128)} %param.11) | copy-start | bytes 786436
  24.2 6.2 %copy-start.2 = (f32[256,256]{1,0:T(8,128)S(1)}, f32[256,256]{1,0:T(8,128)}, u32[]{:S(2)}) copy-start(f32[256,256]{1,0:T(8,128)} %param.10) | copy-start | bytes 786436
  482.9 12.0 %copy-start.4 = (f32[256,256]{1,0:T(8,128)S(1)}, f32[256,256]{1,0:T(8,128)}, u32[]{:S(2)}) copy-start(f32[256,256]{1,0:T(8,128)} %param.11) | copy-start | bytes 786436
  494.9 7.9 %copy-start.5 = (f32[128,256]{1,0:T(8,128)S(1)}, f32[128,256]{1,0:T(8,128)}, u32[]{:S(2)}) copy-start(f32[128,256]{1,0:T(8,128)} %get-tuple-element.5) | copy-start | bytes 393220

commit v2 on v1

--- a/solution.py
+++ b/solution.py
@@ -9,8 +9,8 @@
 
 field_scale = 0.6
 QUARTERS = 4
-MAX_CHUNKS = 16
-AHEAD = 3
+MAX_CHUNKS = 32
+AHEAD = 6
 VMEM_BYTES = 67043328
 HIGH = lax.Precision.HIGH
 
@@ -26,9 +26,10 @@
 
 
 def kernel(
-    group, chunks, q_hbm, cnt_hbm, exp_hbm, lh, ll, th, tl, out_hbm, acc,
-    own, f0, f1, res, wgt, b0, b1,
+    group, chunks, q_hbm, cnt_hbm, exp_hbm, w_hbm, lh, ll, th, tl, out_hbm, density,
+    own, f0, f1, res, wgt, b0, b1, acc, prior, held, near, far,
     send_in, recv_p, recv_c, recv_e, send_z, recv_f0, recv_f1, recv_b0, recv_b1, send_g, recv_g,
+    held_sem, send_near, recv_near, send_far, recv_far,
 ):
     slab = lax.axis_index("slab")
     quarter = slab // group
@@ -49,6 +50,9 @@
     pl.semaphore_wait(barrier, group + QUARTERS - 2)
 
     acc[...] = jnp.zeros_like(acc)
+    prior[...] = jnp.zeros_like(prior)
+    depth = held.shape[0]
+    lanes = density.shape[1]
 
     def part(chunk):
         return pl.ds(chunk * step, step)
@@ -165,6 +169,31 @@
         if q == 1:
             remote(own.at[part(chunk)], f0.at[part(chunk)], send_z.at[0], recv_f0.at[chunk], device(2, place))
 
+    def fetch(chunk):
+        return pltpu.make_async_copy(w_hbm.at[pl.ds(chunk * depth, depth)], held, held_sem)
+
+    def square():
+        values = held[...]
+        prior[...] += jnp.sum((values * values).reshape(depth // 8, 8, values.shape[1]), axis=0)
+
+    def fold(tile):
+        return sum(tile[:, k * lanes : (k + 1) * lanes] for k in range(tile.shape[1] // lanes))
+
+    def send_sum_near():
+        cells = jnp.sum(acc[...].reshape(rows // 8, 8, acc.shape[1]), axis=0)
+        near[place] = fold(cells - 0.5 * prior[...])
+        for j in range(1, group):
+            remote(near.at[place], near.at[place], send_near, recv_near, device(quarter, lax.rem(place + j, group)))
+
+    def send_sum_far():
+        if group > 1:
+            others = near.at[pl.ds(0, group - 1)]
+            await_bytes(others, send_near)
+            await_bytes(others, recv_near)
+        far[quarter] = jnp.sum(near[...], axis=0)
+        for j in range(1, QUARTERS):
+            remote(far.at[quarter], far.at[quarter], send_far, recv_far, device(lax.rem(quarter + j, QUARTERS), place))
+
     ahead = min(AHEAD, chunks)
     for chunk in range(ahead):
         spread(chunk)
@@ -173,6 +202,10 @@
     backward_lag = (4, 3, 3, 2)
 
     def turn(i, carry):
+        @pl.when(i < chunks)
+        def _():
+            fetch(i).start()
+
         @pl.when(i + ahead < chunks)
         def _():
             spread(i + ahead)
@@ -191,9 +224,27 @@
                 backward(q, i - backward_lag[q])
                 collect(i - backward_lag[q])
 
+        @pl.when(i < chunks)
+        def _():
+            fetch(i).wait()
+            square()
+
+        @pl.when(i == chunks + max(forward_lag) - 1)
+        def _():
+            send_sum_near()
+
+        @pl.when(i == chunks + max(forward_lag))
+        def _():
+            send_sum_far()
+
         return carry
 
     lax.fori_loop(0, chunks + max(backward_lag), turn, 0)
+
+    others = far.at[pl.ds(0, QUARTERS - 1)]
+    await_bytes(others, send_far)
+    await_bytes(others, recv_far)
+    density[...] = jnp.sum(far[...], axis=0)
 
     away = pl.ds(0, (group - 1) * lines)
     if group > 1:
@@ -205,13 +256,14 @@
     await_bytes(out_hbm, recv_g)
 
 
-def exchange(partly, counts, exposure, east, group):
+def exchange(partly, counts, exposure, whitened, east, group):
     lines = partly.shape[0] // group
     rows = partly.shape[1] * group
     times = partly.shape[2]
     chunks = min(MAX_CHUNKS, lines)
     rounded = lax.reduce_precision(east, 8, 7)
     high, low = rounded.astype(jnp.bfloat16), (east - rounded).astype(jnp.bfloat16)
+    depth = whitened.shape[0] // chunks
     whole = lambda: pltpu.VMEM((lines, rows, times), jnp.float32)
     any_space = pl.BlockSpec(memory_space=pl.ANY)
     in_vmem = pl.BlockSpec(memory_space=pltpu.VMEM)
@@ -220,36 +272,42 @@
         functools.partial(kernel, group, chunks),
         out_shape=(
             jax.ShapeDtypeStruct(partly.shape, jnp.float32),
-            jax.ShapeDtypeStruct((rows, times), jnp.float32),
+            jax.ShapeDtypeStruct((8, 128), jnp.float32),
         ),
-        in_specs=[any_space] * 3 + [in_vmem] * 4,
+        in_specs=[any_space] * 4 + [in_vmem] * 4,
         out_specs=(any_space, in_vmem),
         scratch_shapes=[whole() for _ in range(7)]
+        + [
+            pltpu.VMEM((rows, times), jnp.float32),
+            pltpu.VMEM((8, times), jnp.float32),
+            pltpu.VMEM((depth, times), jnp.float32),
+            pltpu.VMEM((group, 8, 128), jnp.float32),
+            pltpu.VMEM((QUARTERS, 8, 128), jnp.float32),
+        ]
         + [dma((3,))]
         + [dma((chunks,)) for _ in range(3)]
         + [dma((2,))]
         + [dma((chunks,)) for _ in range(4)]
-        + [dma, dma],
+        + [dma] * 7,
         compiler_params=pltpu.CompilerParams(
             collective_id=0, has_side_effects=True, vmem_limit_bytes=VMEM_BYTES
         ),
-    )(partly, counts, exposure, high, low, high.T, low.T)
+    )(partly, counts, exposure, whitened, high, low, high.T, low.T)
 
 
 def per_device(whitened, counts, exposure, cholesky_east, cholesky_north, cholesky_time):
     slabs = lax.axis_size("slab")
     cell_count = whitened.shape[0] * whitened.shape[1] * whitened.shape[2]
-    prior_term = -0.5 * jnp.sum(whitened * whitened)
     partly = jnp.einsum("abc,tc->abt", whitened, cholesky_time, precision=HIGH)
     partly = jnp.einsum("abt,yb->yat", partly, cholesky_north, precision=HIGH)
     counts_lines = jnp.transpose(counts.astype(jnp.float32), (1, 0, 2))
     exposure_lines = jnp.transpose(exposure.astype(jnp.float32), (1, 0, 2))
-    adjoint, terms = exchange(partly, counts_lines, exposure_lines, cholesky_east, slabs // QUARTERS)
+    flat = jnp.reshape(whitened, (-1, whitened.shape[2]))
+    adjoint, terms = exchange(partly, counts_lines, exposure_lines, flat, cholesky_east, slabs // QUARTERS)
     adjoint = jnp.einsum("yat,yb->abt", adjoint, cholesky_north, precision=HIGH)
     adjoint = jnp.einsum("abt,tc->abc", adjoint, cholesky_time, precision=HIGH)
     gradient = field_scale * adjoint - whitened
-    total_sum = lax.psum(jnp.sum(terms) + prior_term, "slab")
-    density = total_sum / (cell_count * slabs)
+    density = jnp.sum(terms) / (cell_count * slabs)
     return (gradient, jnp.reshape(density, (1,)))
 
 

time: 544 us -> 482 us (0.89)
  blocking collectives: 29 us -> 0 us
  Pallas kernels: 436 us -> 412 us
    psum x1 -> x0, blocking collectives: 29 us -> none  [per_device(): total_sum = lax.psum(jnp.sum(terms) + prior_term, 'slab')]
    pallas_call x1, Pallas kernels: 436 us -> 412 us  [exchange(): pl.pallas_call(functools.partial(kernel, group, chunks), out_shape=(jax.S...]
    reduce_sum x2 -> x1, other arithmetic: 6.77 us -> 1.28 us  [per_device(): density = jnp.sum(terms) / (cell_count * slabs)]
where the time goes in v2:
time: 482 us; the launch traced here: 481 us
  Pallas kernels  412 us (85%)
  matrix products  31.7 us (7%)
  other arithmetic  21.2 us (4%)
  local copies, waits for them, and re-layouts  14.1 us (3%)
    pallas_call x1, Pallas kernels, exchange(): pl.pallas_call(functools.partial(kernel, group, chunks), out_shape=(jax.S...  412 us
    transpose x1, other arithmetic, per_device(): exposure_lines = jnp.transpose(exposure.astype(jnp.float32), (1, 0, 2))  19.8 us
    dot_general x1, matrix products, per_device(): adjoint = jnp.einsum('yat,yb->abt', adjoint, cholesky_north, precision=HIGH)  11.9 us
    dot_general x1, local copies, waits for them, and re-layouts, per_device(): partly = jnp.einsum('abt,yb->yat', partly, cholesky_north, precision=HIGH)  10.3 us

profile of v2, /device:TPU:1, one launch (start us, length us, event | category | flops | bytes accessed | tf_op | source)
XLA Modules:
  0.0 481.2 jit_solution(14475088810043997346)
XLA Ops:
  0.6 1.6 copy.11
  2.2 0.2 fusion.8
  2.4 0.0 copy-start
  2.4 0.0 copy-start.1
  2.4 1.2 copy.14.ll
  3.5 1.1 copy.13.lh
  4.6 0.0 copy-start.2
  4.6 6.1 %fusion.13 = f32[32,256,256]{1,2,0:T(8,128)S(1)} fusion(f32[32,256,256]{2,1,0:T(8,128)} %param.6, f32[256,256]{1,0:T(8,128)} %param.11), kind=kOutput, calls=%fused_computation.16 | convolution fusion | flops 3221225472 | bytes 17039360 | tf_op jit(solution)/shard_map/abc,tc->abt/dot_general | solution.py:301
  10.7 0.0 copy-done
  10.8 0.0 copy-done.1
  10.8 0.0 copy-done.2
  10.8 5.7 %fusion.10 = f32[32,256,256]{2,1,0:T(8,128)} fusion(f32[32,256,256]{1,2,0:T(8,128)S(1)} %fusion.13, f32[256,256]{1,0:T(8,128)S(1)} %copy-done.2), kind=kOutput, calls=%fused_computation.13 | convolution fusion | flops 3221225472 | bytes 17039360 | tf_op jit(solution)/shard_map/abt,yb->yat/dot_general | solution.py:302
  16.5 10.3 %copy.8 = f32[32,256,256]{1,0,2:T(8,128)} copy(f32[32,256,256]{2,1,0:T(8,128)} %fusion.10) | data formatting | bytes 16777216 | tf_op jit(solution)/shard_map/abt,yb->yat/dot_general | solution.py:302
  26.8 19.8 %fusion.4 = (f32[256,32,256]{2,1,0:T(8,128)}, f32[256,32,256]{2,1,0:T(8,128)}) fusion(s32[32,256,256]{2,1,0:T(8,128)} %param.8, s32[32,256,256]{2,1,0:T(8,128)} %param.7), kind=kLoop, calls=%fused_computation.5 | loop fusion | flops 4194304 | bytes 33554432 | tf_op jit(solution)/shard_map/transpose | solution.py:304
  46.5 411.7 %shard_map.77 = (f32[256,32,256]{2,1,0:T(8,128)}, f32[8,128]{1,0:T(8,128)}) custom-call(f32[256,32,256]{2,1,0:T(8,128)} %bitcast.27, f32[256,32,256]{2,1,0:T(8,128)} %get-tuple-element.9.cnt_hbm, f32[256,32,256]{2,1,0:T(8,128)} %get-tuple-element.8.exp_hbm, f32[8192,256]{1,0:T(8,128)} %bitcast.26, bf16[512,512]{1,0:T(8,128)(2,1)} %copy.13.lh, ...), custom_call_target="tpu_custom_call" | custom-call | tf_op jit(solution)/shard_map/pallas_call | solution.py:271
  458.2 1.3 reduce_sum.9
  460.2 0.0 copy-start.3
  460.2 11.9 %fusion.2 = f32[32,256,256]{1,2,0:T(8,128)S(1)} fusion(f32[256,32,256]{2,1,0:T(8,128)} %get-tuple-element.4, f32[256,256]{1,0:T(8,128)} %param.10), kind=kOutput, calls=%fused_computation.2 | convolution fusion | flops 3221225472 | bytes 17039360 | tf_op jit(solution)/shard_map/yat,yb->abt/dot_general | solution.py:307
  472.1 0.0 copy-done.3
  472.2 7.9 %multiply_subtract_fusion = f32[32,256,256]{2,1,0:T(8,128)} fusion(f32[32,256,256]{2,1,0:T(8,128)} %param.6, f32[32,256,256]{1,2,0:T(8,128)S(1)} %fusion.2, f32[256,256]{1,0:T(8,128)S(1)} %copy-done.3), kind=kOutput, calls=%fused_computation.8 | convolution fusion | flops 3225419776 | bytes 25427968 | tf_op jit(solution)/shard_map/abt,tc->abc/dot_general | solution.py:308
Async XLA Ops:
  2.4 8.4 %copy-start = (bf16[512,512]{0,1:T(8,128)(2,1)}, bf16[512,512]{0,1:T(8,128)(2,1)S(1)}, u32[]{:S(2)}) copy-start(bf16[512,512]{0,1:T(8,128)(2,1)S(1)} %get-tuple-element.6) | copy-start | bytes 1572868
  2.4 8.4 %copy-start.1 = (bf16[512,512]{0,1:T(8,128)(2,1)}, bf16[512,512]{0,1:T(8,128)(2,1)S(1)}, u32[]{:S(2)}) copy-start(bf16[512,512]{0,1:T(8,128)(2,1)S(1)} %get-tuple-element.7) | copy-start | bytes 1572868
  4.6 6.2 %copy-start.2 = (f32[256,256]{1,0:T(8,128)S(1)}, f32[256,256]{1,0:T(8,128)}, u32[]{:S(2)}) copy-start(f32[256,256]{1,0:T(8,128)} %param.10) | copy-start | bytes 786436
  460.2 12.0 %copy-start.3 = (f32[256,256]{1,0:T(8,128)S(1)}, f32[256,256]{1,0:T(8,128)}, u32[]{:S(2)}) copy-start(f32[256,256]{1,0:T(8,128)} %param.11) | copy-start | bytes 786436

commit v3 on v2

--- a/solution.py
+++ b/solution.py
@@ -9,8 +9,8 @@
 
 field_scale = 0.6
 QUARTERS = 4
-MAX_CHUNKS = 32
-AHEAD = 6
+MAX_CHUNKS = 64
+AHEAD = 12
 VMEM_BYTES = 67043328
 HIGH = lax.Precision.HIGH
 

time: 482 us -> 471 us (0.977)
  Pallas kernels: 412 us -> 401 us
    pallas_call x1, Pallas kernels: 412 us -> 401 us  [exchange(): pl.pallas_call(functools.partial(kernel, group, chunks), out_shape=(jax.S...]
where the time goes in v3:
time: 471 us; the launch traced here: 470 us
  Pallas kernels  401 us (85%)
  matrix products  31.7 us (7%)
  other arithmetic  21.2 us (5%)
  local copies, waits for them, and re-layouts  14.1 us (3%)
    pallas_call x1, Pallas kernels, exchange(): pl.pallas_call(functools.partial(kernel, group, chunks), out_shape=(jax.S...  401 us
    transpose x1, other arithmetic, per_device(): exposure_lines = jnp.transpose(exposure.astype(jnp.float32), (1, 0, 2))  19.8 us
    dot_general x1, matrix products, per_device(): adjoint = jnp.einsum('yat,yb->abt', adjoint, cholesky_north, precision=HIGH)  11.9 us
    dot_general x1, local copies, waits for them, and re-layouts, per_device(): partly = jnp.einsum('abt,yb->yat', partly, cholesky_north, precision=HIGH)  10.3 us

profile of v3, /device:TPU:1, one launch (start us, length us, event | category | flops | bytes accessed | tf_op | source)
XLA Modules:
  0.0 470.0 jit_solution(1475614074988825163)
XLA Ops:
  0.6 1.6 copy.11
  2.2 0.2 fusion.8
  2.4 0.0 copy-start
  2.4 0.0 copy-start.1
  2.4 1.2 copy.14.ll
  3.5 1.1 copy.13.lh
  4.6 0.0 copy-start.2
  4.6 6.1 %fusion.13 = f32[32,256,256]{1,2,0:T(8,128)S(1)} fusion(f32[32,256,256]{2,1,0:T(8,128)} %param.6, f32[256,256]{1,0:T(8,128)} %param.11), kind=kOutput, calls=%fused_computation.16 | convolution fusion | flops 3221225472 | bytes 17039360 | tf_op jit(solution)/shard_map/abc,tc->abt/dot_general | solution.py:301
  10.7 0.0 copy-done
  10.8 0.0 copy-done.1
  10.8 0.0 copy-done.2
  10.8 5.7 %fusion.10 = f32[32,256,256]{2,1,0:T(8,128)} fusion(f32[32,256,256]{1,2,0:T(8,128)S(1)} %fusion.13, f32[256,256]{1,0:T(8,128)S(1)} %copy-done.2), kind=kOutput, calls=%fused_computation.13 | convolution fusion | flops 3221225472 | bytes 17039360 | tf_op jit(solution)/shard_map/abt,yb->yat/dot_general | solution.py:302
  16.5 10.3 %copy.8 = f32[32,256,256]{1,0,2:T(8,128)} copy(f32[32,256,256]{2,1,0:T(8,128)} %fusion.10) | data formatting | bytes 16777216 | tf_op jit(solution)/shard_map/abt,yb->yat/dot_general | solution.py:302
  26.8 19.8 %fusion.4 = (f32[256,32,256]{2,1,0:T(8,128)}, f32[256,32,256]{2,1,0:T(8,128)}) fusion(s32[32,256,256]{2,1,0:T(8,128)} %param.8, s32[32,256,256]{2,1,0:T(8,128)} %param.7), kind=kLoop, calls=%fused_computation.5 | loop fusion | flops 4194304 | bytes 33554432 | tf_op jit(solution)/shard_map/transpose | solution.py:304
  46.5 400.5 %shard_map.77 = (f32[256,32,256]{2,1,0:T(8,128)}, f32[8,128]{1,0:T(8,128)}) custom-call(f32[256,32,256]{2,1,0:T(8,128)} %bitcast.27, f32[256,32,256]{2,1,0:T(8,128)} %get-tuple-element.9.cnt_hbm, f32[256,32,256]{2,1,0:T(8,128)} %get-tuple-element.8.exp_hbm, f32[8192,256]{1,0:T(8,128)} %bitcast.26, bf16[512,512]{1,0:T(8,128)(2,1)} %copy.13.lh, ...), custom_call_target="tpu_custom_call" | custom-call | tf_op jit(solution)/shard_map/pallas_call | solution.py:271
  447.1 1.3 reduce_sum.9
  449.0 0.0 copy-start.3
  449.0 11.9 %fusion.2 = f32[32,256,256]{1,2,0:T(8,128)S(1)} fusion(f32[256,32,256]{2,1,0:T(8,128)} %get-tuple-element.4, f32[256,256]{1,0:T(8,128)} %param.10), kind=kOutput, calls=%fused_computation.2 | convolution fusion | flops 3221225472 | bytes 17039360 | tf_op jit(solution)/shard_map/yat,yb->abt/dot_general | solution.py:307
  461.0 0.0 copy-done.3
  461.0 7.9 %multiply_subtract_fusion = f32[32,256,256]{2,1,0:T(8,128)} fusion(f32[32,256,256]{2,1,0:T(8,128)} %param.6, f32[32,256,256]{1,2,0:T(8,128)S(1)} %fusion.2, f32[256,256]{1,0:T(8,128)S(1)} %copy-done.3), kind=kOutput, calls=%fused_computation.8 | convolution fusion | flops 3225419776 | bytes 25427968 | tf_op jit(solution)/shard_map/abt,tc->abc/dot_general | solution.py:308
Async XLA Ops:
  2.4 8.4 %copy-start = (bf16[512,512]{0,1:T(8,128)(2,1)}, bf16[512,512]{0,1:T(8,128)(2,1)S(1)}, u32[]{:S(2)}) copy-start(bf16[512,512]{0,1:T(8,128)(2,1)S(1)} %get-tuple-element.6) | copy-start | bytes 1572868
  2.4 8.4 %copy-start.1 = (bf16[512,512]{0,1:T(8,128)(2,1)}, bf16[512,512]{0,1:T(8,128)(2,1)S(1)}, u32[]{:S(2)}) copy-start(bf16[512,512]{0,1:T(8,128)(2,1)S(1)} %get-tuple-element.7) | copy-start | bytes 1572868
  4.6 6.2 %copy-start.2 = (f32[256,256]{1,0:T(8,128)S(1)}, f32[256,256]{1,0:T(8,128)}, u32[]{:S(2)}) copy-start(f32[256,256]{1,0:T(8,128)} %param.10) | copy-start | bytes 786436
  449.0 12.0 %copy-start.3 = (f32[256,256]{1,0:T(8,128)S(1)}, f32[256,256]{1,0:T(8,128)}, u32[]{:S(2)}) copy-start(f32[256,256]{1,0:T(8,128)} %param.11) | copy-start | bytes 786436

commit v4 on v3

--- a/solution.py
+++ b/solution.py
@@ -19,6 +19,11 @@
     high = values.astype(jnp.bfloat16)
     low = (values - high.astype(jnp.float32)).astype(jnp.bfloat16)
     return high, low
+
+
+def halves(matrix):
+    rounded = lax.reduce_precision(matrix, 8, 7)
+    return rounded.astype(jnp.bfloat16), (matrix - rounded).astype(jnp.bfloat16)
 
 
 def dot(left, right):
@@ -256,13 +261,46 @@
     await_bytes(out_hbm, recv_g)
 
 
+def prepare_kernel(w_ref, cnt_ref, exp_ref, th, tl, nh, nl, q_ref, cnt_out, exp_out, held):
+    for a in range(w_ref.shape[0]):
+        x_high, x_low = split(w_ref[a])
+        partly = dot(x_high, th[...]) + (dot(x_low, th[...]) + dot(x_high, tl[...]))
+        x_high, x_low = split(partly)
+        held[a] = dot(nh[...], x_high) + (dot(nh[...], x_low) + dot(nl[...], x_high))
+
+    def turn(i, carry):
+        at = pl.ds(pl.multiple_of(i * 8, 8), 8)
+        q_ref[at] = jnp.swapaxes(held[:, at, :], 0, 1)
+        cnt_out[at] = jnp.swapaxes(cnt_ref[:, at, :].astype(jnp.float32), 0, 1)
+        exp_out[at] = jnp.swapaxes(exp_ref[:, at, :].astype(jnp.float32), 0, 1)
+        return carry
+
+    lax.fori_loop(0, w_ref.shape[1] // 8, turn, 0, unroll=2)
+
+
+def prepare(whitened, counts, exposure, north, time):
+    planes, lines, times = whitened.shape
+    block = 8
+    taken = pl.BlockSpec((block, lines, times), lambda i: (i, 0, 0))
+    given = pl.BlockSpec((lines, block, times), lambda i: (0, i, 0))
+    fixed = [pl.BlockSpec((extent, extent), lambda i: (0, 0)) for extent in (times, times, lines, lines)]
+    return pl.pallas_call(
+        prepare_kernel,
+        grid=(planes // block,),
+        out_shape=[jax.ShapeDtypeStruct((lines, planes, times), jnp.float32)] * 3,
+        in_specs=[taken] * 3 + fixed,
+        out_specs=[given] * 3,
+        scratch_shapes=[pltpu.VMEM((block, lines, times), jnp.float32)],
+        compiler_params=pltpu.CompilerParams(vmem_limit_bytes=VMEM_BYTES),
+    )(whitened, counts, exposure, *halves(time.T), *halves(north))
+
+
 def exchange(partly, counts, exposure, whitened, east, group):
     lines = partly.shape[0] // group
     rows = partly.shape[1] * group
     times = partly.shape[2]
     chunks = min(MAX_CHUNKS, lines)
-    rounded = lax.reduce_precision(east, 8, 7)
-    high, low = rounded.astype(jnp.bfloat16), (east - rounded).astype(jnp.bfloat16)
+    high, low = halves(east)
     depth = whitened.shape[0] // chunks
     whole = lambda: pltpu.VMEM((lines, rows, times), jnp.float32)
     any_space = pl.BlockSpec(memory_space=pl.ANY)
@@ -298,10 +336,7 @@
 def per_device(whitened, counts, exposure, cholesky_east, cholesky_north, cholesky_time):
     slabs = lax.axis_size("slab")
     cell_count = whitened.shape[0] * whitened.shape[1] * whitened.shape[2]
-    partly = jnp.einsum("abc,tc->abt", whitened, cholesky_time, precision=HIGH)
-    partly = jnp.einsum("abt,yb->yat", partly, cholesky_north, precision=HIGH)
-    counts_lines = jnp.transpose(counts.astype(jnp.float32), (1, 0, 2))
-    exposure_lines = jnp.transpose(exposure.astype(jnp.float32), (1, 0, 2))
+    partly, counts_lines, exposure_lines = prepare(whitened, counts, exposure, cholesky_north, cholesky_time)
     flat = jnp.reshape(whitened, (-1, whitened.shape[2]))
     adjoint, terms = exchange(partly, counts_lines, exposure_lines, flat, cholesky_east, slabs // QUARTERS)
     adjoint = jnp.einsum("yat,yb->abt", adjoint, cholesky_north, precision=HIGH)

time: 471 us -> 455 us (0.966)
  Pallas kernels: 401 us -> 424 us
  other arithmetic: 21.2 us -> 3.24 us
  matrix products: 31.7 us -> 19.8 us
  local copies, waits for them, and re-layouts: 14.1 us -> 5.51 us
    pallas_call x0 -> x1, Pallas kernels: none -> 23.1 us  [prepare(): pl.pallas_call(prepare_kernel, grid=(planes // block,), out_shape=[jax.Sh...]
    transpose x1 -> x0, other arithmetic: 19.8 us -> none  [per_device(): exposure_lines = jnp.transpose(exposure.astype(jnp.float32), (1, 0, 2))]
    dot_general x2 -> x0, matrix products: 11.9 us -> none  [the longest x1 6.14 us: per_device(): partly = jnp.einsum('abc,tc->abt', whitened, cholesky_time, precision=HIGH)]
    dot_general x1 -> x0, local copies, waits for them, and re-layouts: 10.3 us -> none  [per_device(): partly = jnp.einsum('abt,yb->yat', partly, cholesky_north, precision=HIGH)]
where the time goes in v4:
time: 455 us
  Pallas kernels  424 us (93%)
  matrix products  19.8 us (4%)
  local copies, waits for them, and re-layouts  5.51 us (1%)
    pallas_call x1, Pallas kernels, exchange(): pl.pallas_call(functools.partial(kernel, group, chunks), out_shape=(jax.S...  401 us
    pallas_call x1, Pallas kernels, prepare(): pl.pallas_call(prepare_kernel, grid=(planes // block,), out_shape=[jax.Sh...  23.1 us
    dot_general x1, matrix products, per_device(): adjoint = jnp.einsum('yat,yb->abt', adjoint, cholesky_north, precision=HIGH)  11.9 us

profile of v4, /device:TPU:1, one launch (start us, length us, event | category | flops | bytes accessed | tf_op | source)
XLA Modules:
  0.0 454.7 jit_solution(4697614092045580017)
XLA Ops:
  0.6 1.1 copy.8
  1.7 1.8 fusion.7
  3.5 1.6 copy.9
  5.1 0.2 fusion.6
  5.2 0.0 copy-start
  5.3 0.0 copy-start.1
  5.3 0.8 copy-done
  6.0 1.0 copy.12.ll
  7.1 0.0 copy-done.1
  7.1 1.1 copy.11.lh
  8.1 23.1 %shard_map.77 = (f32[256,32,256]{2,1,0:T(8,128)}, f32[256,32,256]{2,1,0:T(8,128)}, f32[256,32,256]{2,1,0:T(8,128)}) custom-call(f32[32,256,256]{2,1,0:T(8,128)} %w_ref.1, s32[32,256,256]{2,1,0:T(8,128)} %cnt_ref.1, s32[32,256,256]{2,1,0:T(8,128)} %exp_ref.1, bf16[256,256]{1,0:T(8,128)(2,1)} %get-tuple-element.17.th, bf16[256,256]{1,0:T(8,128)(2,1)} %get-tuple-element.16.tl, ...), custom_call_target="tpu_custom_call" | custom-call | tf_op jit(solution)/shard_map/pallas_call | solution.py:287
  31.3 400.5 %shard_map.78 = (f32[256,32,256]{2,1,0:T(8,128)}, f32[8,128]{1,0:T(8,128)}) custom-call(f32[256,32,256]{2,1,0:T(8,128)} %get-tuple-element.7.q_hbm, f32[256,32,256]{2,1,0:T(8,128)} %get-tuple-element.8.cnt_hbm, f32[256,32,256]{2,1,0:T(8,128)} %get-tuple-element.9.exp_hbm, f32[8192,256]{1,0:T(8,128)} %bitcast.18, bf16[512,512]{1,0:T(8,128)(2,1)} %copy.11.lh, ...), custom_call_target="tpu_custom_call" | custom-call | tf_op jit(solution)/shard_map/pallas_call | solution.py:309
  431.8 1.3 reduce_sum.9
  433.7 0.0 copy-start.2
  433.8 11.9 %fusion.2 = f32[32,256,256]{1,2,0:T(8,128)S(1)} fusion(f32[256,32,256]{2,1,0:T(8,128)} %get-tuple-element.10, f32[256,256]{1,0:T(8,128)} %param.10), kind=kOutput, calls=%fused_computation.2 | convolution fusion | flops 3221225472 | bytes 17039360 | tf_op jit(solution)/shard_map/yat,yb->abt/dot_general | solution.py:342
  445.7 0.0 copy-done.2
  445.7 7.9 %multiply_subtract_fusion = f32[32,256,256]{2,1,0:T(8,128)} fusion(f32[32,256,256]{2,1,0:T(8,128)} %w_ref.1, f32[32,256,256]{1,2,0:T(8,128)S(1)} %fusion.2, f32[256,256]{1,0:T(8,128)S(1)} %copy-done.2), kind=kOutput, calls=%fused_computation.4 | convolution fusion | flops 3225419776 | bytes 25427968 | tf_op jit(solution)/shard_map/abt,tc->abc/dot_general | solution.py:343
Async XLA Ops:
  5.2 0.8 copy-start
  5.3 1.8 copy-start.1
  433.7 12.0 %copy-start.2 = (f32[256,256]{1,0:T(8,128)S(1)}, f32[256,256]{1,0:T(8,128)}, u32[]{:S(2)}) copy-start(f32[256,256]{1,0:T(8,128)} %param.11) | copy-start | bytes 786436
